TPU v7x, 128 devices: a whole 4x4x4 slice. The times are simulated.
128 devices in a mesh: seq: 16 (over z, y_hi, core), chan: 8 (over y_lo, x).
Axes of the slice: x: 4, y: 4 (y_hi: 2, y_lo: 2; y = y_hi * 2 + y_lo), z: 4, core: 2. Of those that a mesh axis runs over, the one named last changes fastest.
Arguments:
- values: bfloat16 [4096, 4096], P('seq', 'chan'), may hold values from -6 to 6
- gates: bfloat16 [4096, 4096], P('seq', 'chan'), may hold values from -6 to 6
- filters: bfloat16 [1024, 4096], P(None, 'chan'), may hold values from -2 to 2
- skip: float32 [4096], P('chan'), may hold values from -4 to 4
- out_weight: bfloat16 [4096, 4096], P(('seq', 'chan')), may hold values from -0.09375 to 0.09375
Outputs:
- projected: bfloat16 [4096, 4096], P(('seq', 'chan'))
All inputs are finite; a program needn't handle non-finite values.
Results may differ from a plain program's by a relative error of at most 0.009.
Values may be sent and summed in bfloat16 or wider, within the bound.
A program may use at most 128 MiB of HBM per device.

v0:
```python
import numpy as np

import jax
import jax.numpy as jnp
from jax import lax
from jax.sharding import PartitionSpec as P


def dft_tables(block):
    size = 2 * block
    freq = (np.arange(block) + 0.5)[:, None]
    angle = 2.0 * np.pi * freq * np.arange(size)[None, :] / size
    forward = np.concatenate([np.cos(angle), -np.sin(angle)], axis=0)
    late = angle[:, block:]
    backward = np.concatenate([np.cos(late), -np.sin(late)], axis=0).T / block
    return forward, backward


def from_behind(value, axis, steps):
    count = lax.axis_size(axis)
    return lax.ppermute(value, axis, [(source, source + steps) for source in range(count - steps)])


def dot(a, b):
    return jnp.dot(a, b, preferred_element_type=jnp.float32)


def body(values, gates, filters, skip, out_weight):
    block = values.shape[0]
    taps = filters.shape[0] // block
    forward, backward = dft_tables(block)
    forward = jnp.asarray(forward, jnp.bfloat16)
    backward = jnp.asarray(backward, jnp.bfloat16)
    part = lax.all_to_all(out_weight, "chan", split_axis=1, concat_axis=0, tiled=True)
    columns = lax.all_gather(part, "seq", axis=0, tiled=True)
    blocks = [values] + [from_behind(values, "seq", step) for step in range(1, taps + 1)]
    real = 0.0
    imag = 0.0
    for j in range(taps):
        kernel = dot(forward[:, :block], filters[j * block : (j + 1) * block])
        window = dot(forward, jnp.concatenate([blocks[j + 1], blocks[j]], axis=0))
        kr, ki = kernel[:block], kernel[block:]
        wr, wi = window[:block], window[block:]
        real = real + kr * wr - ki * wi
        imag = imag + kr * wi + ki * wr
    spectrum = jnp.concatenate([real, imag], axis=0).astype(jnp.bfloat16)
    filtered = dot(backward, spectrum) + skip[None, :] * values.astype(jnp.float32)
    gated = (gates.astype(jnp.float32) * filtered).astype(jnp.bfloat16)
    rows = lax.all_gather(gated, "chan", axis=1, tiled=True)
    summed = dot(rows, columns).astype(jnp.bfloat16)
    return lax.all_to_all(summed, "chan", split_axis=0, concat_axis=1, tiled=True)


def solution(mesh):
    in_specs = (
        P("seq", "chan"),
        P("seq", "chan"),
        P(None, "chan"),
        P("chan"),
        P(("seq", "chan"), None),
    )
    out_specs = P(("seq", "chan"), None)
    return jax.shard_map(body, mesh=mesh, in_specs=in_specs, out_specs=out_specs, check_vma=False)
```

profile of v0, /device:TPU:1, one launch (start us, length us, event | category | flops | bytes accessed | tf_op | source)
XLA Modules:
  0.0 166.8 jit_solution(8608560338992499461)
XLA Ops:
  6.5 0.0 all-gather.3.cloned.1.call-start
  6.5 6.5 %collective-permute-start.1 = (bf16[256,512]{1,0:T(8,128)(2,1)}, bf16[256,512]{1,0:T(8,128)(2,1)}, u32[]{:S(2)}, u32[]{:S(2)}) collective-permute-start(bf16[256,512]{1,0:T(8,128)(2,1)} %param.7), channel_id=1, source_target_pairs={{0,16},{8,24},{16,32},{24,40},{32,48},{40,56},{48,64},{56,72},{64,... | collective-permute-start | bytes 786440 | tf_op jit(solution)/shard_map/ppermute | solution.py:21
  13.0 4.4 %collective-permute-start.2 = (bf16[256,512]{1,0:T(8,128)(2,1)}, bf16[256,512]{1,0:T(8,128)(2,1)}, u32[]{:S(2)}, u32[]{:S(2)}) collective-permute-start(bf16[256,512]{1,0:T(8,128)(2,1)} %param.7), channel_id=1, source_target_pairs={{0,24},{8,32},{16,40},{24,48},{32,56},{40,64},{48,72},{56,80},{64,... | collective-permute-start | bytes 786440 | tf_op jit(solution)/shard_map/ppermute | solution.py:21
  17.4 4.0 %collective-permute-start = (bf16[256,512]{1,0:T(8,128)(2,1)}, bf16[256,512]{1,0:T(8,128)(2,1)}, u32[]{:S(2)}, u32[]{:S(2)}) collective-permute-start(bf16[256,512]{1,0:T(8,128)(2,1)} %param.7), channel_id=1, source_target_pairs={{0,8},{8,16},{16,24},{24,32},{32,40},{40,48},{48,56},{56,64},{64,7... | collective-permute-start | bytes 786440 | tf_op jit(solution)/shard_map/ppermute | solution.py:21
  21.4 3.6 %collective-permute-start.3 = (bf16[256,512]{1,0:T(8,128)(2,1)}, bf16[256,512]{1,0:T(8,128)(2,1)}, u32[]{:S(2)}, u32[]{:S(2)}) collective-permute-start(bf16[256,512]{1,0:T(8,128)(2,1)} %param.7), channel_id=1, source_target_pairs={{0,32},{8,40},{16,48},{24,56},{32,64},{40,72},{48,80},{56,88},{64,... | collective-permute-start | bytes 786440 | tf_op jit(solution)/shard_map/ppermute | solution.py:21
  25.0 1.3 fusion.10
  26.3 1.3 fusion.4
  27.6 1.3 fusion.6
  29.0 0.0 copy-done
  29.0 2.2 %fusion.8 = f32[512,512]{1,0:T(8,128)} fusion(bf16[512,256]{1,0:T(8,128)(2,1)S(1)} %copy-done, bf16[1024,512]{1,0:T(8,128)(2,1)} %param.9), kind=kOutput, calls=%fused_computation.17 | convolution fusion | flops 134217728 | bytes 1572864 | tf_op jit(solution)/shard_map/dot_general | solution.py:25
  31.2 1.8 %copy.15 = bf16[256,512]{0,1:T(8,128)(2,1)} copy(bf16[256,512]{1,0:T(8,128)(2,1)} %param.7) | data formatting | bytes 524288 | tf_op args[0]
  33.0 1.8 %copy.14 = bf16[256,512]{0,1:T(8,128)(2,1)} copy(bf16[256,512]{1,0:T(8,128)(2,1)} %param.8) | data formatting | bytes 524288 | tf_op args[1]
  34.8 1.4 fusion.13
  36.2 0.0 collective-permute-done
  36.2 1.2 convolution_add_fusion.3
  37.4 0.0 copy-done.2
  37.4 1.2 fusion.14
  38.7 0.0 collective-permute-done.1
  38.7 1.2 convolution_add_fusion.2
  39.9 0.0 copy-start.1
  39.9 0.0 copy-start.7
  40.0 1.3 fusion.15
  41.3 0.0 collective-permute-done.2
  41.3 1.2 convolution_add_fusion.1
  42.6 0.0 copy-start.3
  42.6 0.0 copy-start.4
  42.6 0.0 copy-start.6
  42.6 0.0 copy-start.8
  42.6 1.3 fusion.16
  43.9 0.0 collective-permute-done.3
  43.9 1.2 convolution_add_fusion
  45.2 0.0 copy-done.1
  45.2 0.0 copy-start.5
  45.2 1.0 fusion.12
  46.2 0.0 copy-done.3
  46.2 0.0 copy-done.4
  46.2 0.0 copy-done.6
  46.2 0.0 copy-done.8
  46.2 1.7 %fusion.3 = bf16[256,512]{0,1:T(8,128)(2,1)} fusion(f32[512,256]{1,0:T(8,128)S(1)} %fusion.12, bf16[256,256]{1,0:T(8,128)(2,1)S(1)} %copy-done.6, bf16[256,512]{0,1:T(8,128)(2,1)S(1)} %copy-done.3, bf16[256,512]{0,1:T(8,128)(2,1)S(1)} %copy-done.4, f32[512]{0:T(512)S(1)} %copy-done.8, f32[512,512]{1,0:T(8,128)S(1)} %convolution_add_fusion, ...), kind=kOutput, calls=%fused_computation.8 | convolution fusion | flops 70123520 | bytes 9832448 | tf_op jit(solution)/shard_map/dot_general | solution.py:25
  47.9 0.0 all-gather.3.cloned.1.call-update
  48.0 0.0 all-gather.5.cloned.1.call-start
  48.0 12.4 %all_to_all.38 = bf16[32,8,512]{2,0,1:T(8,128)(2,1)} all-to-all(bf16[32,8,512]{2,0,1:T(8,128)(2,1)S(1)} %bitcast.45), channel_id=1, replica_groups=mesh['seq'=16,'chan'=8] {'chan'}, dimensions={1} | all-to-all | bytes 524288 | tf_op jit(solution)/shard_map/all_to_all | solution.py:34
  60.4 0.0 all-gather.5.cloned.1.call-update
  60.5 22.0 %all-gather.3.cloned.1.call-done = bf16[256,4096]{0,1:T(8,128)(2,1)} async-done(((bf16[256,512]{0,1:T(8,128)(2,1)}), bf16[256,4096]{0,1:T(8,128)(2,1)}) %all-gather.3.cloned.1.call-update) | async-done | bytes 2097168 | tf_op jit(solution)/shard_map/all_gather | solution.py:49
  82.5 61.5 %all-gather.5.cloned.1.call-done = bf16[4096,512]{1,0:T(8,128)(2,1)} async-done(((bf16[256,512]{1,0:T(8,128)(2,1)}), bf16[4096,512]{1,0:T(8,128)(2,1)}) %all-gather.5.cloned.1.call-update) | async-done | bytes 4194320 | tf_op jit(solution)/shard_map/all_gather | solution.py:35
  144.0 4.1 %convolution_convert_fusion = bf16[256,512]{1,0:T(8,128)(2,1)S(1)} fusion(bf16[256,4096]{0,1:T(8,128)(2,1)} %all-gather.3.cloned.1.call-done, bf16[4096,512]{1,0:T(8,128)(2,1)} %all-gather.5.cloned.1.call-done), kind=kOutput, calls=%fused_computation.9 | convolution fusion | flops 1073872896 | bytes 6553600 | tf_op jit(solution)/shard_map/dot_general | solution.py:25
  148.0 11.2 %all_to_all.39 = bf16[8,32,512]{2,1,0:T(8,128)(2,1)S(1)} all-to-all(bf16[8,32,512]{2,1,0:T(8,128)(2,1)S(1)} %bitcast.47), channel_id=1, replica_groups=mesh['seq'=16,'chan'=8] {'chan'}, dimensions={0} | all-to-all | bytes 524288 | tf_op jit(solution)/shard_map/all_to_all | solution.py:51
  159.3 0.7 copy.19
  (5 shorter events, 0.0 us)
Async XLA Ops:
  6.5 22.4 %copy-start = (bf16[512,256]{1,0:T(8,128)(2,1)S(1)}, bf16[512,256]{1,0:T(8,128)(2,1)}, u32[]{:S(2)}) copy-start(bf16[512,256]{1,0:T(8,128)(2,1)} %constant.7) | copy-start | bytes 786436
  6.5 75.9 %all-gather.3.cloned.1.call-start = ((), (), s32[]{:S(2)}) async-start(), calls=%async_computation.2 | async-start | bytes 2359296 | tf_op jit(solution)/shard_map/all_gather | solution.py:49
  6.5 32.1 %collective-permute-start.1 = (bf16[256,512]{1,0:T(8,128)(2,1)}, bf16[256,512]{1,0:T(8,128)(2,1)}, u32[]{:S(2)}, u32[]{:S(2)}) collective-permute-start(bf16[256,512]{1,0:T(8,128)(2,1)} %param.7), channel_id=1, source_target_pairs={{0,16},{8,24},{16,32},{24,40},{32,48},{40,56},{48,64},{56,72},{64,... | collective-permute-start | bytes 786440 | tf_op jit(solution)/shard_map/ppermute | solution.py:21
  13.0 28.3 %collective-permute-start.2 = (bf16[256,512]{1,0:T(8,128)(2,1)}, bf16[256,512]{1,0:T(8,128)(2,1)}, u32[]{:S(2)}, u32[]{:S(2)}) collective-permute-start(bf16[256,512]{1,0:T(8,128)(2,1)} %param.7), channel_id=1, source_target_pairs={{0,24},{8,32},{16,40},{24,48},{32,56},{40,64},{48,72},{56,80},{64,... | collective-permute-start | bytes 786440 | tf_op jit(solution)/shard_map/ppermute | solution.py:21
  17.4 18.8 %collective-permute-start = (bf16[256,512]{1,0:T(8,128)(2,1)}, bf16[256,512]{1,0:T(8,128)(2,1)}, u32[]{:S(2)}, u32[]{:S(2)}) collective-permute-start(bf16[256,512]{1,0:T(8,128)(2,1)} %param.7), channel_id=1, source_target_pairs={{0,8},{8,16},{16,24},{24,32},{32,40},{40,48},{48,56},{56,64},{64,7... | collective-permute-start | bytes 786440 | tf_op jit(solution)/shard_map/ppermute | solution.py:21
  21.4 22.5 %collective-permute-start.3 = (bf16[256,512]{1,0:T(8,128)(2,1)}, bf16[256,512]{1,0:T(8,128)(2,1)}, u32[]{:S(2)}, u32[]{:S(2)}) collective-permute-start(bf16[256,512]{1,0:T(8,128)(2,1)} %param.7), channel_id=1, source_target_pairs={{0,32},{8,40},{16,48},{24,56},{32,64},{40,72},{48,80},{56,88},{64,... | collective-permute-start | bytes 786440 | tf_op jit(solution)/shard_map/ppermute | solution.py:21
  34.8 2.6 %copy-start.2 = (bf16[512,256]{1,0:T(8,128)(2,1)S(1)}, bf16[512,256]{1,0:T(8,128)(2,1)}, u32[]{:S(2)}) copy-start(bf16[512,256]{1,0:T(8,128)(2,1)} %constant.8) | copy-start | bytes 786436
  39.9 5.2 %copy-start.1 = (f32[512,512]{1,0:T(8,128)S(1)}, f32[512,512]{1,0:T(8,128)}, u32[]{:S(2)}) copy-start(f32[512,512]{1,0:T(8,128)} %fusion.8) | copy-start | bytes 3145732
  39.9 5.2 %copy-start.7 = (bf16[256,256]{1,0:T(8,128)(2,1)S(1)}, bf16[256,256]{1,0:T(8,128)(2,1)}, u32[]{:S(2)}) copy-start(bf16[256,256]{1,0:T(8,128)(2,1)} %constant.9) | copy-start | bytes 393220
  42.6 3.6 %copy-start.3 = (bf16[256,512]{0,1:T(8,128)(2,1)S(1)}, bf16[256,512]{0,1:T(8,128)(2,1)}, u32[]{:S(2)}) copy-start(bf16[256,512]{0,1:T(8,128)(2,1)} %copy.15) | copy-start | bytes 786436
  42.6 3.6 %copy-start.4 = (bf16[256,512]{0,1:T(8,128)(2,1)S(1)}, bf16[256,512]{0,1:T(8,128)(2,1)}, u32[]{:S(2)}) copy-start(bf16[256,512]{0,1:T(8,128)(2,1)} %copy.14) | copy-start | bytes 786436
  42.6 3.6 %copy-start.6 = (bf16[256,256]{1,0:T(8,128)(2,1)S(1)}, bf16[256,256]{1,0:T(8,128)(2,1)}, u32[]{:S(2)}) copy-start(bf16[256,256]{1,0:T(8,128)(2,1)} %constant.10) | copy-start | bytes 393220
  42.6 3.6 %copy-start.8 = (f32[512]{0:T(512)S(1)}, f32[512]{0:T(512)}, u32[]{:S(2)}) copy-start(f32[512]{0:T(512)} %param.10) | copy-start | bytes 6148
  45.2 2.8 %copy-start.5 = (bf16[32,4096]{1,0:T(8,128)(2,1)S(1)}, bf16[32,4096]{1,0:T(8,128)(2,1)}, u32[]{:S(2)}) copy-start(bf16[32,4096]{1,0:T(8,128)(2,1)} %param.11) | copy-start | bytes 786436
  48.0 96.0 %all-gather.5.cloned.1.call-start = ((), (), s32[]{:S(2)}) async-start(), calls=%async_computation.3 | async-start | bytes 4456448 | tf_op jit(solution)/shard_map/all_gather | solution.py:35
Sparse Core Ops, SparseCore 0:
  48.1 34.3 all-gather.2
  84.9 58.9 all-gather.4
where the time goes:
time: 167 us
  waiting for transfers between devices  83.5 us (50%)
  blocking collectives  23.6 us (14%)
  matrix products  23.1 us (14%)
  starting transfers between devices  18.5 us (11%)
  between operations  13.6 us (8%)
  local copies, waits for them, and re-layouts  4.39 us (3%)
    all_gather x1, waiting for transfers between devices, body(): columns = lax.all_gather(part, 'seq', axis=0, tiled=True)  61.5 us
    dot_general x15, matrix products, dot(): return jnp.dot(a, b, preferred_element_type=jnp.float32)  23.1 us
    all_gather x1, waiting for transfers between devices, body(): rows = lax.all_gather(gated, 'chan', axis=1, tiled=True)  22 us
    ppermute x4, starting transfers between devices, from_behind(): lax.ppermute(value, axis, [(source, source + steps) for source in range(c...  18.5 us
    all_to_all x1, blocking collectives, body(): lax.all_to_all(out_weight, 'chan', split_axis=1, concat_axis=0, tiled=True)  12.4 us
    all_to_all x1, blocking collectives, body(): lax.all_to_all(summed, 'chan', split_axis=0, concat_axis=1, tiled=True)  11.2 us
    unnamed x20, local copies, waits for them, and re-layouts  3.65 us
  transfers between devices with their start and end apart: 6, of which 2 were waited for; matrix products, arithmetic and copies ran while one was open for 11% of the time, Pallas kernels for 0%

commit v1 on v0

v1 whole, which is shorter than its diff:
```python
import functools

import numpy as np

import jax
import jax.numpy as jnp
from jax import lax
from jax.experimental import pallas as pl
from jax.experimental.pallas import tpu as pltpu
from jax.sharding import PartitionSpec as P

MESH = pl.DeviceIdType.MESH
CHUNKS = 2
BLOCK = 256
WIDTH = 512
PART = WIDTH // CHUNKS
TAPS = 4
PEERS = 8
GROUPS = 16
ROWS = 32
HALF = BLOCK // 2
STRIP = 32


def dft_tables(block):
    size = 2 * block
    freq = (np.arange(block) + 0.5)[:, None]
    angle = 2.0 * np.pi * freq * np.arange(size)[None, :] / size
    forward = np.concatenate([np.cos(angle), -np.sin(angle)], axis=0)
    late = angle[:, block:]
    backward = np.concatenate([np.cos(late), -np.sin(late)], axis=0).T / block
    return forward, backward


def dot(a, b):
    return jnp.dot(a, b, preferred_element_type=jnp.float32)


def kernel(
    values, gates, filters, skip, weight, forward, backward, out,
    xbuf, gbuf, fbuf, tables, inverse, kern, zbuf, ybuf, abuf, wbuf, acc, obuf,
    send_sem, recv_sem, local_sem,
):
    s = lax.axis_index("seq")
    c = lax.axis_index("chan")
    z, yh, k = s // 4, (s // 2) % 2, s % 2
    yl, x = c // 4, c % 4

    def seq_at(dz, dyh, dk):
        return ((z + dz + 4) % 4) * 4 + ((yh + dyh) % 2) * 2 + (k + dk) % 2

    def chan_at(dyl, dx):
        return ((yl + dyl) % 2) * 4 + (x + dx + 4) % 4

    def seq_dev(index):
        return {"seq": index, "chan": c}

    def chan_dev(index):
        return {"seq": s, "chan": index}

    z_up, z_down = seq_dev(seq_at(1, 0, 0)), seq_dev(seq_at(-1, 0, 0))
    y_far, mate = seq_dev(seq_at(0, 1, 0)), seq_dev(seq_at(0, 0, 1))
    x_up, x_down = chan_dev(chan_at(0, 1)), chan_dev(chan_at(0, -1))
    y_near = chan_dev(chan_at(1, 0))
    ahead, behind = (s + 2) % GROUPS, (s + GROUPS - 2) % GROUPS

    pending = []

    def send(src, dst, device):
        index = len(pending)
        copy = pltpu.make_async_remote_copy(
            src_ref=src, dst_ref=dst, send_sem=send_sem.at[index], recv_sem=recv_sem.at[index],
            device_id=device, device_id_type=MESH,
        )
        copy.start()
        pending.append(copy)
        return copy

    locals_started = []

    def fetch(src, dst):
        copy = pltpu.make_async_copy(src, dst, local_sem.at[len(locals_started)])
        copy.start()
        locals_started.append(copy)
        return copy

    barrier = pltpu.get_barrier_semaphore()
    sources = [chan_dev((c + i) % PEERS) for i in range(1, PEERS)]
    sources += [z_up, z_down, y_far, mate, seq_dev(behind)]
    for device in sources:
        pl.semaphore_signal(barrier, inc=1, device_id=device, device_id_type=MESH)

    def cols(q):
        return pl.ds(q * PART, PART)

    def lag(n):
        return pl.ds((TAPS - n) * BLOCK, BLOCK)

    get_filters = fetch(filters, fbuf)
    get_forward = fetch(forward, tables)
    get_values = [fetch(values.at[:, cols(q)], xbuf.at[q, lag(0)]) for q in range(CHUNKS)]
    get_backward = fetch(backward, inverse)
    get_gates = fetch(gates, gbuf)

    def wcols(index):
        return pl.ds(pl.multiple_of(index * WIDTH, WIDTH), WIDTH)

    def rows_of(index):
        return pl.ds(pl.multiple_of(index * ROWS, ROWS), ROWS)

    get_weight = fetch(weight.at[:, wcols(c)], wbuf.at[s, rows_of(c)])

    pl.semaphore_wait(barrier, len(sources))

    far, near = [], []
    for q in range(CHUNKS):
        near.append(send(values.at[:, cols(q)], xbuf.at[q, lag(2)], seq_dev(ahead)))
        far.append(send(values.at[:, cols(q)], xbuf.at[q, lag(4)], z_up))
    shares = []
    for i in range(1, PEERS):
        peer = (c + i) % PEERS
        shares.append(send(weight.at[:, wcols(peer)], wbuf.at[s, rows_of(c)], chan_dev(peer)))

    get_filters.wait()
    get_forward.wait()

    def spectrum(j, _):
        taps = fbuf[pl.ds(pl.multiple_of(j * BLOCK, BLOCK), BLOCK), :]
        kern[j] = dot(tables[:, :BLOCK], taps)
        return 0

    lax.fori_loop(0, TAPS, spectrum, 0)

    get_weight.wait()
    for copy in shares:
        copy.wait_recv()

    def wpiece(dz, dyh, dk=0):
        return wbuf.at[seq_at(dz, dyh, dk)]

    def whalf(dz, dyh, lower):
        return wbuf.at[seq_at(dz, dyh, 0), pl.ds(HALF * lower, HALF)]

    def wsend(ref, device):
        return send(ref, ref, device)

    w_up = wsend(wpiece(0, 0), z_up)
    w_down = wsend(wpiece(0, 0), z_down)
    w_far = wsend(wpiece(0, 0), y_far)
    w_mate = [wsend(wpiece(0, 0), mate)]

    for copy in get_values:
        copy.wait()
    get_backward.wait()
    get_gates.wait()

    def window(q, j):
        old = xbuf[q, lag(j + 1), :]
        new = xbuf[q, lag(j), :]
        old = jnp.where(s >= j + 1, old, jnp.zeros_like(old))
        new = jnp.where(s >= j, new, jnp.zeros_like(new))
        return jnp.concatenate([old, new], axis=0)

    def convolve(q):
        near[q].wait_recv()
        src = (TAPS - 2 * k) * BLOCK
        first = send(xbuf.at[q, pl.ds(pl.multiple_of(src, BLOCK), BLOCK)], xbuf.at[q, lag(1)], mate)
        far[q].wait_recv()
        src = (TAPS - 2 - 2 * k) * BLOCK
        second = send(xbuf.at[q, pl.ds(pl.multiple_of(src, BLOCK), BLOCK)], xbuf.at[q, lag(3)], mate)
        first.wait_recv()
        second.wait_recv()
        for j in range(TAPS):
            zbuf[j] = dot(tables[...], window(q, j))

        def combine(i, _):
            re = pl.ds(pl.multiple_of(i * STRIP, STRIP), STRIP)
            im = pl.ds(pl.multiple_of(i * STRIP + BLOCK, STRIP), STRIP)
            real = jnp.zeros((STRIP, PART), jnp.float32)
            imag = jnp.zeros((STRIP, PART), jnp.float32)
            for j in range(TAPS):
                kr, ki = kern[j, re, cols(q)], kern[j, im, cols(q)]
                wr, wi = zbuf[j, re, :], zbuf[j, im, :]
                real = real + kr * wr - ki * wi
                imag = imag + kr * wi + ki * wr
            ybuf[re, :] = real.astype(jnp.bfloat16)
            ybuf[im, :] = imag.astype(jnp.bfloat16)
            return 0

        lax.fori_loop(0, BLOCK // STRIP, combine, 0)
        now = xbuf[q, lag(0), :].astype(jnp.float32)
        filtered = dot(inverse[...], ybuf[...]) + skip[:, cols(q)] * now
        abuf[c, q] = (gbuf[:, cols(q)].astype(jnp.float32) * filtered).astype(jnp.bfloat16)

    def apiece(q, dyl, dx):
        return abuf.at[chan_at(dyl, dx), q]

    def ahalf(q, dyl, dx, lower):
        return abuf.at[chan_at(dyl, dx), q, pl.ds(HALF * lower, HALF)]

    a_up, a_down, a_near = [], [], []

    def spread(q):
        own = apiece(q, 0, 0)
        a_up.append(send(own, own, x_up))
        a_down.append(send(own, own, x_down))
        a_near.append(send(own, own, y_near))

    a_up2, a_down2, a_nup, a_ndown, a_nfar = [], [], [], [], []

    def relay(q):
        a_up[q].wait_recv()
        ref = ahalf(q, 0, -1, 0)
        a_up2.append(send(ref, ref, x_up))
        a_down[q].wait_recv()
        ref = ahalf(q, 0, 1, 1)
        a_down2.append(send(ref, ref, x_down))
        a_near[q].wait_recv()
        ref = apiece(q, 1, 0)
        a_nup.append(send(ref, ref, x_up))
        a_ndown.append(send(ref, ref, x_down))

    def relay_far(q):
        a_up2[q].wait_recv()
        a_down2[q].wait_recv()
        ref = apiece(q, 0, 2)
        a_nfar.append(send(ref, ref, y_near))

    convolve(0)
    spread(0)
    w_up.wait_recv()
    w_up2 = wsend(whalf(-1, 0, 0), z_up)
    w_mate.append(wsend(wpiece(-1, 0), mate))
    w_down.wait_recv()
    w_down2 = wsend(whalf(1, 0, 1), z_down)
    w_mate.append(wsend(wpiece(1, 0), mate))
    convolve(1)
    spread(1)
    w_far.wait_recv()
    w_fup = wsend(wpiece(0, 1), z_up)
    w_fdown = wsend(wpiece(0, 1), z_down)
    w_mate.append(wsend(wpiece(0, 1), mate))
    relay(0)
    relay(1)
    w_up2.wait_recv()
    w_down2.wait_recv()
    w_mate.append(wsend(wpiece(2, 0), mate))
    relay_far(0)
    relay_far(1)
    w_fup.wait_recv()
    w_fup2 = wsend(whalf(-1, 1, 0), z_up)
    w_mate.append(wsend(wpiece(-1, 1), mate))
    w_fdown.wait_recv()
    w_fdown2 = wsend(whalf(1, 1, 1), z_down)
    w_mate.append(wsend(wpiece(1, 1), mate))
    w_fup2.wait_recv()
    w_fdown2.wait_recv()
    w_mate.append(wsend(wpiece(2, 1), mate))
    for copy in w_mate:
        copy.wait_recv()

    def project(q, dyl, dx, start=False):
        origin = chan_at(dyl, dx)
        row = q * PART
        term = dot(
            abuf[origin, q], wbuf[2 * origin + row // BLOCK, pl.ds(row % BLOCK, PART), :]
        )
        if start:
            acc[...] = term
        else:
            acc[...] += term

    for q in range(CHUNKS):
        project(q, 0, 0, start=q == 0)
        project(q, 0, -1)
        project(q, 0, 1)
        project(q, 1, 0)
        project(q, 0, 2)
    for q in range(CHUNKS):
        a_nup[q].wait_recv()
        project(q, 1, -1)
        a_ndown[q].wait_recv()
        project(q, 1, 1)
        a_nfar[q].wait_recv()
        project(q, 1, 2)

    obuf[...] = acc[...].astype(jnp.bfloat16)
    mine = pltpu.make_async_copy(
        obuf.at[rows_of(c)], out.at[:, wcols(c)], local_sem.at[len(locals_started)]
    )
    mine.start()
    results = []
    for i in range(1, PEERS):
        peer = (c + i) % PEERS
        results.append(send(obuf.at[rows_of(peer)], out.at[:, wcols(c)], chan_dev(peer)))
    mine.wait()
    for copy in results:
        copy.wait_recv()
    for copy in pending:
        copy.wait_send()


MESSAGES = 4 * CHUNKS + 7 + 17 + 8 * CHUNKS + 7


def body(values, gates, filters, skip, out_weight):
    forward, backward = dft_tables(BLOCK)
    forward = jnp.asarray(forward, jnp.bfloat16)
    backward = jnp.asarray(backward, jnp.bfloat16)
    anywhere = pl.BlockSpec(memory_space=pl.ANY)
    local = pl.BlockSpec(memory_space=pltpu.VMEM)
    bf16, f32 = jnp.bfloat16, jnp.float32
    return pl.pallas_call(
        kernel,
        out_shape=jax.ShapeDtypeStruct((ROWS, PEERS * WIDTH), bf16),
        in_specs=[anywhere, anywhere, anywhere, local, anywhere, anywhere, anywhere],
        out_specs=anywhere,
        scratch_shapes=[
            pltpu.VMEM((CHUNKS, (TAPS + 1) * BLOCK, PART), bf16),
            pltpu.VMEM((BLOCK, WIDTH), bf16),
            pltpu.VMEM((TAPS * BLOCK, WIDTH), bf16),
            pltpu.VMEM((2 * BLOCK, 2 * BLOCK), bf16),
            pltpu.VMEM((BLOCK, 2 * BLOCK), bf16),
            pltpu.VMEM((TAPS, 2 * BLOCK, WIDTH), f32),
            pltpu.VMEM((TAPS, 2 * BLOCK, PART), f32),
            pltpu.VMEM((2 * BLOCK, PART), bf16),
            pltpu.VMEM((PEERS, CHUNKS, BLOCK, PART), bf16),
            pltpu.VMEM((GROUPS, BLOCK, WIDTH), bf16),
            pltpu.VMEM((BLOCK, WIDTH), f32),
            pltpu.VMEM((BLOCK, WIDTH), bf16),
            pltpu.SemaphoreType.DMA((MESSAGES,)),
            pltpu.SemaphoreType.DMA((MESSAGES,)),
            pltpu.SemaphoreType.DMA((8,)),
        ],
        compiler_params=pltpu.CompilerParams(
            collective_id=0, has_side_effects=True, vmem_limit_bytes=48 << 20
        ),
    )(values, gates, filters, skip.reshape(1, -1), out_weight, forward, backward)


def solution(mesh):
    in_specs = (
        P("seq", "chan"),
        P("seq", "chan"),
        P(None, "chan"),
        P("chan"),
        P(("seq", "chan"), None),
    )
    out_specs = P(("seq", "chan"), None)
    return jax.shard_map(body, mesh=mesh, in_specs=in_specs, out_specs=out_specs, check_vma=False)
```

time: 167 us -> 60.3 us (0.36)
  waiting for transfers between devices: 83.5 us -> 0 us
  Pallas kernels: 0 us -> 52.5 us
  blocking collectives: 23.6 us -> 0 us
  matrix products: 23.1 us -> 0 us
  starting transfers between devices: 18.5 us -> 0 us
  between operations: 13.6 us -> 0.02 us
  local copies, waits for them, and re-layouts: 4.39 us -> 7.45 us
    all_gather x2 -> x0, waiting for transfers between devices: 83.5 us -> none  [the longest x1 61.5 us: body(): columns = lax.all_gather(part, 'seq', axis=0, tiled=True)]
    pallas_call x0 -> x1, Pallas kernels: none -> 52.5 us  [body(): pl.pallas_call(kernel, out_shape=jax.ShapeDtypeStruct((ROWS, PEERS * WIDT...]
    all_to_all x2 -> x0, blocking collectives: 23.6 us -> none  [the longest x1 12.4 us: body(): lax.all_to_all(out_weight, 'chan', split_axis=1, concat_axis=0, tiled=True)]
    dot_general x15 -> x0, matrix products: 23.1 us -> none  [dot(): return jnp.dot(a, b, preferred_element_type=jnp.float32)]
    ppermute x4 -> x0, starting transfers between devices: 18.5 us -> none  [from_behind(): lax.ppermute(value, axis, [(source, source + steps) for source in range(c...]
    unnamed x20 -> x15, local copies, waits for them, and re-layouts: 3.65 us -> 7.45 us
  transfers between devices with their start and end apart: 6 -> 0, of which waited for: 2 -> 0; matrix products, arithmetic and copies ran while one was open for 11% -> 0% of each run, Pallas kernels for 0% -> 0%
where the time goes in v1:
time: 60.3 us; the launch traced here: 59.9 us
  Pallas kernels  52.5 us (87%)
  local copies, waits for them, and re-layouts  7.45 us (12%)
    pallas_call x1, Pallas kernels, body(): pl.pallas_call(kernel, out_shape=jax.ShapeDtypeStruct((ROWS, PEERS * WIDT...  52.5 us
    unnamed x15, local copies, waits for them, and re-layouts  7.45 us

profile of v1, /device:TPU:1, one launch (start us, length us, event | category | flops | bytes accessed | tf_op | source)
XLA Modules:
  0.0 59.9 jit_solution(7259920460299498488)
XLA Ops:
  0.0 0.0 copy-start
  0.0 1.2 %copy-done = bf16[1024,512]{1,0:T(8,128)(2,1)S(1)} copy-done((bf16[1024,512]{1,0:T(8,128)(2,1)S(1)}, bf16[1024,512]{1,0:T(8,128)(2,1)}, u32[]{:S(2)}) %copy-start) | copy-done | bytes 1048600
  1.2 0.0 copy-start.1
  1.2 1.0 %copy-done.1 = bf16[512,512]{1,0:T(8,128)(2,1)S(1)} copy-done((bf16[512,512]{1,0:T(8,128)(2,1)S(1)}, bf16[512,512]{1,0:T(8,128)(2,1)}, u32[]{:S(2)}) %copy-start.1) | copy-done | bytes 524312
  2.3 0.0 copy-start.2
  2.3 0.9 %copy-done.2 = bf16[256,512]{1,0:T(8,128)(2,1)S(1)} copy-done((bf16[256,512]{1,0:T(8,128)(2,1)S(1)}, bf16[256,512]{1,0:T(8,128)(2,1)}, u32[]{:S(2)}) %copy-start.2) | copy-done | bytes 262168
  3.2 0.0 copy-start.3
  3.2 0.9 %copy-done.3 = bf16[256,512]{1,0:T(8,128)(2,1)S(1)} copy-done((bf16[256,512]{1,0:T(8,128)(2,1)S(1)}, bf16[256,512]{1,0:T(8,128)(2,1)}, u32[]{:S(2)}) %copy-start.3) | copy-done | bytes 262168
  4.2 0.0 copy-start.4
  4.2 0.9 %copy-done.4 = bf16[32,4096]{1,0:T(8,128)(2,1)S(1)} copy-done((bf16[32,4096]{1,0:T(8,128)(2,1)S(1)}, bf16[32,4096]{1,0:T(8,128)(2,1)}, u32[]{:S(2)}) %copy-start.4) | copy-done | bytes 262168
  5.1 0.0 copy-start.5
  5.1 0.9 %copy-done.5 = bf16[256,512]{1,0:T(8,128)(2,1)S(1)} copy-done((bf16[256,512]{1,0:T(8,128)(2,1)S(1)}, bf16[256,512]{1,0:T(8,128)(2,1)}, u32[]{:S(2)}) %copy-start.5) | copy-done | bytes 262168
  6.1 0.0 copy-start.6
  6.1 0.7 %copy-done.6 = f32[512]{0:T(512)S(1)} copy-done((f32[512]{0:T(512)S(1)}, f32[512]{0:T(512)}, u32[]{:S(2)}) %copy-start.6) | copy-done | bytes 2072
  6.8 52.5 %shard_map.73 = bf16[32,4096]{1,0:T(8,128)(2,1)S(1)} custom-call(bf16[256,512]{1,0:T(8,128)(2,1)S(1)} %copy-done.2, bf16[256,512]{1,0:T(8,128)(2,1)S(1)} %copy-done.3, bf16[1024,512]{1,0:T(8,128)(2,1)S(1)} %copy-done, f32[1,512]{1,0:T(1,128)S(1)} %bitcast.1, bf16[32,4096]{1,0:T(8,128)(2,1)S(1)} %copy-done.4, bf16[512,512]{1,0:T(8,128)(2,1)S(1)} %copy-done.1, ...), custom_call_target="tpu_custom_call" | custom-call | tf_op jit(solution)/shard_map/pallas_call | solution.py:313
  59.2 0.7 %copy.9 = bf16[32,4096]{1,0:T(8,128)(2,1)} copy(bf16[32,4096]{1,0:T(8,128)(2,1)S(1)} %shard_map.73) | data formatting | bytes 524288
Async XLA Ops:
  0.0 1.2 %copy-start = (bf16[1024,512]{1,0:T(8,128)(2,1)S(1)}, bf16[1024,512]{1,0:T(8,128)(2,1)}, u32[]{:S(2)}) copy-start(bf16[1024,512]{1,0:T(8,128)(2,1)} %filters.1) | copy-start | bytes 3145732
  1.2 1.0 %copy-start.1 = (bf16[512,512]{1,0:T(8,128)(2,1)S(1)}, bf16[512,512]{1,0:T(8,128)(2,1)}, u32[]{:S(2)}) copy-start(bf16[512,512]{1,0:T(8,128)(2,1)} %constant.4.clone.forward) | copy-start | bytes 1572868
  2.3 0.9 %copy-start.2 = (bf16[256,512]{1,0:T(8,128)(2,1)S(1)}, bf16[256,512]{1,0:T(8,128)(2,1)}, u32[]{:S(2)}) copy-start(bf16[256,512]{1,0:T(8,128)(2,1)} %values.1) | copy-start | bytes 786436
  3.2 0.9 %copy-start.3 = (bf16[256,512]{1,0:T(8,128)(2,1)S(1)}, bf16[256,512]{1,0:T(8,128)(2,1)}, u32[]{:S(2)}) copy-start(bf16[256,512]{1,0:T(8,128)(2,1)} %gates.1) | copy-start | bytes 786436
  4.2 0.9 %copy-start.4 = (bf16[32,4096]{1,0:T(8,128)(2,1)S(1)}, bf16[32,4096]{1,0:T(8,128)(2,1)}, u32[]{:S(2)}) copy-start(bf16[32,4096]{1,0:T(8,128)(2,1)} %weight.1) | copy-start | bytes 786436
  5.1 0.9 %copy-start.5 = (bf16[256,512]{1,0:T(8,128)(2,1)S(1)}, bf16[256,512]{1,0:T(8,128)(2,1)}, u32[]{:S(2)}) copy-start(bf16[256,512]{1,0:T(8,128)(2,1)} %constant.5.clone.backward) | copy-start | bytes 786436
  6.1 0.7 %copy-start.6 = (f32[512]{0:T(512)S(1)}, f32[512]{0:T(512)}, u32[]{:S(2)}) copy-start(f32[512]{0:T(512)} %param.10) | copy-start | bytes 6148

commit v2 on v1

v2 whole, which is shorter than its diff:
```python
import functools

import numpy as np

import jax
import jax.numpy as jnp
from jax import lax
from jax.experimental import pallas as pl
from jax.experimental.pallas import tpu as pltpu
from jax.sharding import PartitionSpec as P

MESH = pl.DeviceIdType.MESH
CHUNKS = 4
BLOCK = 256
WIDTH = 512
PART = WIDTH // CHUNKS
TAPS = 4
PEERS = 8
GROUPS = 16
ROWS = 32
HALF = BLOCK // 2
STRIP = 32
USE_NEAR = True
SCHEDULE = (
    ("f", 0), ("f", 1), ("own",), ("f", 2), ("f", 3), ("cross",),
    ("c", 0), ("s", 0), ("c", 1), ("s", 1), ("wr",), ("c", 2), ("s", 2), ("wo",),
    ("c", 3), ("s", 3), ("r", 0), ("r", 1), ("w2",), ("r", 2), ("R", 0), ("r", 3),
    ("R", 1), ("wro",), ("R", 2), ("R", 3), ("wl",),
)


def dft_tables(block):
    size = 2 * block
    freq = (np.arange(block) + 0.5)[:, None]
    angle = 2.0 * np.pi * freq * np.arange(size)[None, :] / size
    forward = np.concatenate([np.cos(angle), -np.sin(angle)], axis=0)
    late = angle[:, block:]
    backward = np.concatenate([np.cos(late), -np.sin(late)], axis=0).T / block
    return forward, backward


def dot(a, b):
    return jnp.dot(a, b, preferred_element_type=jnp.float32)


def kernel(
    values, gates, filters, skip, weight, forward, backward, out,
    xbuf, gbuf, fbuf, tables, inverse, kern, zbuf, ybuf, abuf, wbuf, acc, obuf,
    send_sem, recv_sem, local_sem,
):
    s = lax.axis_index("seq")
    c = lax.axis_index("chan")
    z, yh, k = s // 4, (s // 2) % 2, s % 2
    yl, x = c // 4, c % 4

    def seq_at(dz, dyh, dk):
        return ((z + dz + 4) % 4) * 4 + ((yh + dyh) % 2) * 2 + (k + dk) % 2

    def chan_at(dyl, dx):
        return ((yl + dyl) % 2) * 4 + (x + dx + 4) % 4

    def seq_dev(index):
        return {"seq": index, "chan": c}

    def chan_dev(index):
        return {"seq": s, "chan": index}

    z_up, z_down = seq_dev(seq_at(1, 0, 0)), seq_dev(seq_at(-1, 0, 0))
    y_far, mate = seq_dev(seq_at(0, 1, 0)), seq_dev(seq_at(0, 0, 1))
    x_up, x_down = chan_dev(chan_at(0, 1)), chan_dev(chan_at(0, -1))
    y_near = chan_dev(chan_at(1, 0))

    pending = []

    def message(src, dst, device):
        index = len(pending)
        copy = pltpu.make_async_remote_copy(
            src_ref=src, dst_ref=dst, send_sem=send_sem.at[index], recv_sem=recv_sem.at[index],
            device_id=device, device_id_type=MESH,
        )
        pending.append(copy)
        return copy

    def send(src, dst, device):
        copy = message(src, dst, device)
        copy.start()
        return copy

    locals_started = []

    def fetch(src, dst):
        copy = pltpu.make_async_copy(src, dst, local_sem.at[len(locals_started)])
        copy.start()
        locals_started.append(copy)
        return copy

    barrier = pltpu.get_barrier_semaphore()
    sources = [chan_dev((c + i) % PEERS) for i in range(1, PEERS)]
    sources += [z_up, z_down, y_far, mate]
    for device in sources:
        pl.semaphore_signal(barrier, inc=1, device_id=device, device_id_type=MESH)

    def cols(q):
        return pl.ds(q * PART, PART)

    def lag(n):
        return pl.ds((TAPS - n) * BLOCK, BLOCK)

    get_filters = fetch(filters, fbuf)
    get_forward = fetch(forward, tables)
    get_values = [fetch(values.at[:, cols(q)], xbuf.at[q, lag(0)]) for q in range(CHUNKS)]
    get_backward = fetch(backward, inverse)
    get_gates = fetch(gates, gbuf)

    def wcols(index):
        return pl.ds(pl.multiple_of(index * WIDTH, WIDTH), WIDTH)

    def rows_of(index):
        return pl.ds(pl.multiple_of(index * ROWS, ROWS), ROWS)

    get_weight = fetch(weight.at[:, wcols(c)], wbuf.at[s, rows_of(c)])

    pl.semaphore_wait(barrier, len(sources))

    far, near, first, second = [], [], [], []
    for q in range(CHUNKS):
        copy = message(values.at[:, cols(q)], xbuf.at[q, lag(4)], z_up)
        pl.when(z < 3)(copy.start)
        far.append(copy)
        src = pl.ds(pl.multiple_of((1 - yh) * TAPS * BLOCK, BLOCK), BLOCK)
        near.append(message(xbuf.at[q, src], xbuf.at[q, lag(2)], y_far))
        src = pl.ds(pl.multiple_of((1 - k) * TAPS * BLOCK, BLOCK), BLOCK)
        dst = pl.ds(pl.multiple_of((3 - 2 * k) * BLOCK, BLOCK), BLOCK)
        first.append(message(xbuf.at[q, src], xbuf.at[q, dst], mate))
        dst = pl.ds(pl.multiple_of((1 + 2 * k) * BLOCK, BLOCK), BLOCK)
        second.append(message(xbuf.at[q, lag(2)], xbuf.at[q, dst], mate))
    shares = []
    for i in range(1, PEERS):
        peer = (c + i) % PEERS
        copy = message(weight.at[:, wcols(peer)], wbuf.at[s, rows_of(c)], chan_dev(peer))
        copy.start()
        shares.append(copy)
    for q in range(CHUNKS):
        get_values[q].wait()
        pl.when(yh == 0)(near[q].start)
        pl.when(k == 0)(first[q].start)

    for n in range(1, TAPS + 1):

        @pl.when(s < n)
        def _():
            for q in range(CHUNKS):
                xbuf[q, lag(n), :] = jnp.zeros((BLOCK, PART), jnp.bfloat16)

    get_filters.wait()
    get_forward.wait()

    def spectrum(j, _):
        taps = fbuf[pl.ds(pl.multiple_of(j * BLOCK, BLOCK), BLOCK), :]
        kern[j] = dot(tables[:, :BLOCK], taps)
        return 0

    lax.fori_loop(0, TAPS, spectrum, 0)
    get_backward.wait()
    get_gates.wait()

    def wpiece(dz, dyh):
        return wbuf.at[seq_at(dz, dyh, 0)]

    def whalf(dz, dyh, lower):
        return wbuf.at[seq_at(dz, dyh, 0), pl.ds(HALF * lower, HALF)]

    w_mate = []

    def to_mate(dz, dyh):
        w_mate.append(send(wpiece(dz, dyh), wpiece(dz, dyh), mate))

    def forward_far(q):
        pl.when(z > 0)(far[q].wait_recv)
        pl.when((yh == 1) & (z > 0))(near[q].start)
        pl.when((k == 1) & (z > 0))(first[q].start)

    def window(q, j):
        return xbuf[q, pl.ds((TAPS - 1 - j) * BLOCK, 2 * BLOCK), :]

    def convolve(q):
        @pl.when(s >= 2)
        def _():
            near[q].wait_recv()
            second[q].start()

        pl.when((k == 1) | (z > 0))(first[q].wait_recv)
        pl.when(s >= 2)(second[q].wait_recv)
        for j in range(TAPS):
            zbuf[j] = dot(tables[...], window(q, j))

        def combine(i, _):
            re = pl.ds(pl.multiple_of(i * STRIP, STRIP), STRIP)
            im = pl.ds(pl.multiple_of(i * STRIP + BLOCK, STRIP), STRIP)
            real = jnp.zeros((STRIP, PART), jnp.float32)
            imag = jnp.zeros((STRIP, PART), jnp.float32)
            for j in range(TAPS):
                kr, ki = kern[j, re, cols(q)], kern[j, im, cols(q)]
                wr, wi = zbuf[j, re, :], zbuf[j, im, :]
                real = real + kr * wr - ki * wi
                imag = imag + kr * wi + ki * wr
            ybuf[re, :] = real.astype(jnp.bfloat16)
            ybuf[im, :] = imag.astype(jnp.bfloat16)
            return 0

        lax.fori_loop(0, BLOCK // STRIP, combine, 0)
        now = xbuf[q, lag(0), :].astype(jnp.float32)
        filtered = dot(inverse[...], ybuf[...]) + skip[:, cols(q)] * now
        abuf[c, :, cols(q)] = (gbuf[:, cols(q)].astype(jnp.float32) * filtered).astype(jnp.bfloat16)

    def apiece(q, dyl, dx):
        return abuf.at[chan_at(dyl, dx), :, cols(q)]

    def ahalf(q, dyl, dx, lower):
        return abuf.at[chan_at(dyl, dx), pl.ds(HALF * lower, HALF), cols(q)]

    def same(ref, device):
        return send(ref, ref, device)

    a_up, a_down, a_near = [], [], []

    def spread(q):
        a_up.append(same(apiece(q, 0, 0), x_up))
        a_down.append(same(apiece(q, 0, 0), x_down))
        a_near.append(same(apiece(q, 0, 0), y_near))

    a_up2, a_down2, a_nup, a_ndown, a_nfar = [], [], [], [], []

    def relay(q):
        a_up[q].wait_recv()
        a_up2.append(same(ahalf(q, 0, -1, 0), x_up))
        a_down[q].wait_recv()
        a_down2.append(same(ahalf(q, 0, 1, 1), x_down))
        a_near[q].wait_recv()
        a_nup.append(same(apiece(q, 1, 0), x_up))
        a_ndown.append(same(apiece(q, 1, 0), x_down))

    def relay_far(q):
        if USE_NEAR:
            a_up2[q].wait_recv()
            a_down2[q].wait_recv()
            a_nfar.append([same(apiece(q, 0, 2), y_near)])
        else:
            a_nup[q].wait_recv()
            up = same(ahalf(q, 1, -1, 0), x_up)
            a_ndown[q].wait_recv()
            a_nfar.append([up, same(ahalf(q, 1, 1, 1), x_down)])

    w = {}

    def w_own():
        get_weight.wait()
        for copy in shares:
            copy.wait_recv()
        w["up"] = same(wpiece(0, 0), z_up)
        w["down"] = same(wpiece(0, 0), z_down)
        to_mate(0, 0)

    def w_cross():
        w["far"] = same(wpiece(0, 0), y_far)

    def w_relay():
        w["down"].wait_recv()
        w["down2"] = same(whalf(1, 0, 1), z_down)
        to_mate(1, 0)
        w["up"].wait_recv()
        w["up2"] = same(whalf(-1, 0, 0), z_up)
        to_mate(-1, 0)

    def w_other():
        w["far"].wait_recv()
        w["fup"] = same(wpiece(0, 1), z_up)
        w["fdown"] = same(wpiece(0, 1), z_down)
        to_mate(0, 1)

    def w_two():
        w["down2"].wait_recv()
        w["up2"].wait_recv()
        to_mate(2, 0)

    def w_relay_other():
        w["fdown"].wait_recv()
        w["fdown2"] = same(whalf(1, 1, 1), z_down)
        to_mate(1, 1)
        w["fup"].wait_recv()
        w["fup2"] = same(whalf(-1, 1, 0), z_up)
        to_mate(-1, 1)

    def w_last():
        w["fdown2"].wait_recv()
        w["fup2"].wait_recv()
        to_mate(2, 1)

    for step in SCHEDULE:
        name, *rest = step
        {
            "f": forward_far, "c": convolve, "s": spread, "r": relay, "R": relay_far,
            "own": w_own, "cross": w_cross, "wr": w_relay, "wo": w_other, "w2": w_two,
            "wro": w_relay_other, "wl": w_last,
        }[name](*rest)
    for copy in w_mate:
        copy.wait_recv()

    def project(dyl, dx, start=False):
        origin = chan_at(dyl, dx)
        term = dot(abuf[origin], wbuf[pl.ds(2 * origin, 2)].reshape(WIDTH, WIDTH))
        if start:
            acc[...] = term
        else:
            acc[...] += term

    project(0, 0, start=True)
    project(0, -1)
    project(0, 1)
    project(1, 0)
    if not USE_NEAR:
        for q in range(CHUNKS):
            a_up2[q].wait_recv()
            a_down2[q].wait_recv()
    project(0, 2)
    if USE_NEAR:
        for q in range(CHUNKS):
            a_nup[q].wait_recv()
            a_ndown[q].wait_recv()
    project(1, -1)
    project(1, 1)
    for group in a_nfar:
        for copy in group:
            copy.wait_recv()
    project(1, 2)

    obuf[...] = acc[...].astype(jnp.bfloat16)
    mine = pltpu.make_async_copy(
        obuf.at[rows_of(c)], out.at[:, wcols(c)], local_sem.at[len(locals_started)]
    )
    mine.start()
    results = []
    for i in range(1, PEERS):
        peer = (c + i) % PEERS
        results.append(send(obuf.at[rows_of(peer)], out.at[:, wcols(c)], chan_dev(peer)))
    mine.wait()
    for copy in results:
        copy.wait_recv()
    for copy in far:
        pl.when(z < 3)(copy.wait_send)
    for copy in near:
        pl.when((yh == 0) | (z > 0))(copy.wait_send)
    for copy in first:
        pl.when((k == 0) | (z > 0))(copy.wait_send)
    for copy in second:
        pl.when(s >= 2)(copy.wait_send)
    for copy in pending:
        if not any(copy is other for other in far + near + first + second):
            copy.wait_send()


MESSAGES = 4 * CHUNKS + 7 + 17 + 9 * CHUNKS + 7


def body(values, gates, filters, skip, out_weight):
    forward, backward = dft_tables(BLOCK)
    forward = jnp.asarray(forward, jnp.bfloat16)
    backward = jnp.asarray(backward, jnp.bfloat16)
    anywhere = pl.BlockSpec(memory_space=pl.ANY)
    local = pl.BlockSpec(memory_space=pltpu.VMEM)
    bf16, f32 = jnp.bfloat16, jnp.float32
    return pl.pallas_call(
        kernel,
        out_shape=jax.ShapeDtypeStruct((ROWS, PEERS * WIDTH), bf16),
        in_specs=[anywhere, anywhere, anywhere, local, anywhere, anywhere, anywhere],
        out_specs=anywhere,
        scratch_shapes=[
            pltpu.VMEM((CHUNKS, (TAPS + 1) * BLOCK, PART), bf16),
            pltpu.VMEM((BLOCK, WIDTH), bf16),
            pltpu.VMEM((TAPS * BLOCK, WIDTH), bf16),
            pltpu.VMEM((2 * BLOCK, 2 * BLOCK), bf16),
            pltpu.VMEM((BLOCK, 2 * BLOCK), bf16),
            pltpu.VMEM((TAPS, 2 * BLOCK, WIDTH), f32),
            pltpu.VMEM((TAPS, 2 * BLOCK, PART), f32),
            pltpu.VMEM((2 * BLOCK, PART), bf16),
            pltpu.VMEM((PEERS, BLOCK, WIDTH), bf16),
            pltpu.VMEM((GROUPS, BLOCK, WIDTH), bf16),
            pltpu.VMEM((BLOCK, WIDTH), f32),
            pltpu.VMEM((BLOCK, WIDTH), bf16),
            pltpu.SemaphoreType.DMA((MESSAGES,)),
            pltpu.SemaphoreType.DMA((MESSAGES,)),
            pltpu.SemaphoreType.DMA((16,)),
        ],
        compiler_params=pltpu.CompilerParams(
            collective_id=0, has_side_effects=True, vmem_limit_bytes=60 * 1024 * 1024
        ),
    )(values, gates, filters, skip.reshape(1, -1), out_weight, forward, backward)


def solution(mesh):
    in_specs = (
        P("seq", "chan"),
        P("seq", "chan"),
        P(None, "chan"),
        P("chan"),
        P(("seq", "chan"), None),
    )
    out_specs = P(("seq", "chan"), None)
    return jax.shard_map(body, mesh=mesh, in_specs=in_specs, out_specs=out_specs, check_vma=False)
```

time: 60.3 us -> 50.4 us (0.84)
  local copies, waits for them, and re-layouts: 7.45 us -> 1.67 us
  Pallas kernels: 52.5 us -> 48.1 us
    unnamed x15 -> x1, local copies, waits for them, and re-layouts: 7.45 us -> 1.67 us
    pallas_call x1, Pallas kernels: 52.5 us -> 48.1 us  [body(): pl.pallas_call(kernel, out_shape=jax.ShapeDtypeStruct((ROWS, PEERS * WIDT...]
where the time goes in v2:
time: 50.4 us; the launch traced here: 49.8 us
  Pallas kernels  48.1 us (95%)
  local copies, waits for them, and re-layouts  1.67 us (3%)
    pallas_call x1, Pallas kernels, body(): pl.pallas_call(kernel, out_shape=jax.ShapeDtypeStruct((ROWS, PEERS * WIDT...  48.1 us
    unnamed x1, local copies, waits for them, and re-layouts  1.67 us

profile of v2, /device:TPU:1, one launch (start us, length us, event | category | flops | bytes accessed | tf_op | source)
XLA Modules:
  0.0 49.8 jit_solution(7620902463444587476)
XLA Ops:
  0.0 48.1 %shard_map.73 = bf16[32,4096]{1,0:T(8,128)(2,1)} custom-call(bf16[256,512]{1,0:T(8,128)(2,1)} %values.1, bf16[256,512]{1,0:T(8,128)(2,1)} %gates.1, bf16[1024,512]{1,0:T(8,128)(2,1)} %filters.1, f32[1,512]{1,0:T(1,128)} %bitcast.1, bf16[32,4096]{1,0:T(8,128)(2,1)} %weight.1, bf16[512,512]{1,0:T(8,128)(2,1)} %constant.4.clone.forward, ...), custom_call_target="tpu_custom_call" | custom-call | tf_op jit(solution)/shard_map/pallas_call | solution.py:372
  48.1 1.7 %copy.9 = bf16[32,4096]{1,0:T(8,128)(2,1)} copy(bf16[32,4096]{1,0:T(8,128)(2,1)} %shard_map.73) | data formatting | bytes 524288

commit v3 on v2

v3 whole, which is shorter than its diff:
```python
import functools

import numpy as np

import jax
import jax.numpy as jnp
from jax import lax
from jax.experimental import pallas as pl
from jax.experimental.pallas import tpu as pltpu
from jax.sharding import PartitionSpec as P

MESH = pl.DeviceIdType.MESH
CHUNKS = 4
BLOCK = 256
WIDTH = 512
PART = WIDTH // CHUNKS
TAPS = 4
PEERS = 8
GROUPS = 16
ROWS = 32
HALF = BLOCK // 2
QUARTER = BLOCK // 4
STRIP = 32
USE_NEAR = True
SHARE, RESULT, WEIGHT, GATED, HALO = range(5)
DIRECT = (0,)
SCHEDULE = (
    ("f", 0), ("f", 1), ("n", 0), ("own",), ("x", 0), ("f", 2),
    ("c", 0), ("s", 0), ("f", 3), ("n", 1), ("x", 1), ("c", 1),
    ("s", 1), ("x", 2), ("n", 2), ("r", 0), ("wr",), ("c", 2),
    ("s", 2), ("x", 3), ("n", 3), ("o", 0), ("c", 3), ("s", 3),
    ("r", 1), ("o", 1), ("wm",), ("r", 2), ("o", 2), ("o", 3),
    ("R", 0), ("u", 0), ("u", 1), ("w2",), ("r", 3), ("R", 1),
    ("d", 2), ("R", 2), ("d", 3), ("R", 3), ("wmo",),
)


def dft_tables(block):
    size = 2 * block
    freq = (np.arange(block) + 0.5)[:, None]
    angle = 2.0 * np.pi * freq * np.arange(size)[None, :] / size
    forward = np.concatenate([np.cos(angle), -np.sin(angle)], axis=0)
    late = angle[:, block:]
    backward = np.concatenate([np.cos(late), -np.sin(late)], axis=0).T / block
    return forward, backward


def dot(a, b):
    return jnp.dot(a, b, preferred_element_type=jnp.float32)


def kernel(
    values, gates, filters, skip, weight, forward, backward, out,
    xbuf, gbuf, fbuf, tables, inverse, kern, zbuf, total, ybuf, abuf, wbuf, acc, obuf,
    send_sem, recv_sem, local_sem,
):
    s = lax.axis_index("seq")
    c = lax.axis_index("chan")
    z, yh, k = s // 4, (s // 2) % 2, s % 2
    yl, x = c // 4, c % 4

    def seq_at(dz, dyh, dk):
        return ((z + dz + 4) % 4) * 4 + ((yh + dyh) % 2) * 2 + (k + dk) % 2

    def chan_at(dyl, dx):
        return ((yl + dyl) % 2) * 4 + (x + dx + 4) % 4

    def seq_dev(index):
        return {"seq": index, "chan": c}

    def chan_dev(index):
        return {"seq": s, "chan": index}

    z_up, z_down = seq_dev(seq_at(1, 0, 0)), seq_dev(seq_at(-1, 0, 0))
    y_far, mate = seq_dev(seq_at(0, 1, 0)), seq_dev(seq_at(0, 0, 1))
    x_up, x_down = chan_dev(chan_at(0, 1)), chan_dev(chan_at(0, -1))
    y_near = chan_dev(chan_at(1, 0))

    used = {"send": 4, "recv": 2}

    def take(name):
        used[name] += 1
        return used[name] - 1

    def message(src, dst, device, kind):
        send_index = take("send") if kind == HALO else kind
        recv_index = kind if kind in (SHARE, RESULT) else take("recv")
        return pltpu.make_async_remote_copy(
            src_ref=src, dst_ref=dst, send_sem=send_sem.at[send_index],
            recv_sem=recv_sem.at[recv_index], device_id=device, device_id_type=MESH,
        )

    def send(src, dst, device, kind):
        copy = message(src, dst, device, kind)
        copy.start()
        return copy

    def drain(ref, sem):
        pltpu.make_async_copy(ref, ref, sem).wait()

    locals_started = []

    def fetch(src, dst):
        copy = pltpu.make_async_copy(src, dst, local_sem.at[len(locals_started)])
        copy.start()
        locals_started.append(copy)
        return copy

    barrier = pltpu.get_barrier_semaphore()
    sources = [chan_dev((c + i) % PEERS) for i in range(1, PEERS)]
    sources += [z_up, z_down, y_far, mate, seq_dev((s + GROUPS - 2) % GROUPS)]
    for device in sources:
        pl.semaphore_signal(barrier, inc=1, device_id=device, device_id_type=MESH)

    def cols(q):
        return pl.ds(q * PART, PART)

    def lag(n):
        return pl.ds((TAPS - n) * BLOCK, BLOCK)

    get_filters = fetch(filters, fbuf.at[pl.ds(BLOCK, TAPS * BLOCK)])
    get_forward = fetch(forward, tables)
    get_values = [fetch(values.at[:, cols(q)], xbuf.at[q, lag(0)]) for q in range(CHUNKS)]
    get_backward = fetch(backward, inverse)
    get_gates = fetch(gates, gbuf)

    def wcols(index):
        return pl.ds(pl.multiple_of(index * WIDTH, WIDTH), WIDTH)

    def rows_of(index):
        return pl.ds(pl.multiple_of(index * ROWS, ROWS), ROWS)

    get_weight = fetch(weight.at[:, wcols(c)], wbuf.at[s, rows_of(c)])

    edge = jnp.zeros((BLOCK, WIDTH), jnp.bfloat16)
    fbuf[:BLOCK, :] = edge
    fbuf[(TAPS + 1) * BLOCK :, :] = edge

    pl.semaphore_wait(barrier, len(sources))

    far, near, first, second = [], [], [], []
    for q in range(CHUNKS):
        copy = message(values.at[:, cols(q)], xbuf.at[q, lag(4)], z_up, HALO)
        pl.when(z < 3)(copy.start)
        far.append(copy)
        if q in DIRECT:
            copy = message(values.at[:, cols(q)], xbuf.at[q, lag(2)], seq_dev((s + 2) % GROUPS), HALO)
            pl.when(s + 2 < GROUPS)(copy.start)
        else:
            src = pl.ds(pl.multiple_of((1 - yh) * TAPS * BLOCK, BLOCK), BLOCK)
            copy = message(xbuf.at[q, src], xbuf.at[q, lag(2)], y_far, HALO)
        near.append(copy)
        src = pl.ds(pl.multiple_of((1 - k) * TAPS * BLOCK, BLOCK), BLOCK)
        dst = pl.ds(pl.multiple_of((3 - 2 * k) * BLOCK, BLOCK), BLOCK)
        first.append(message(xbuf.at[q, src], xbuf.at[q, dst], mate, HALO))
        dst = pl.ds(pl.multiple_of((1 + 2 * k) * BLOCK, BLOCK), BLOCK)
        second.append(message(xbuf.at[q, lag(2)], xbuf.at[q, dst], mate, HALO))
    others = [(1, 2), (1, 1), (1, -1), (0, 2), (1, 0), (0, 1), (0, -1)]
    for dyl, dx in others:
        peer = chan_at(dyl, dx)
        send(weight.at[:, wcols(peer)], wbuf.at[s, rows_of(c)], chan_dev(peer), SHARE)
    for q in range(CHUNKS):
        get_values[q].wait()
        if q not in DIRECT:
            pl.when(yh == 0)(near[q].start)
        pl.when(k == 0)(first[q].start)

    for n in range(1, TAPS + 1):

        @pl.when(s < n)
        def _():
            for q in range(CHUNKS):
                xbuf[q, lag(n), :] = jnp.zeros((BLOCK, PART), jnp.bfloat16)

    get_filters.wait()
    get_forward.wait()

    def spectrum(n, _):
        taps = fbuf[pl.ds(pl.multiple_of(n * BLOCK, BLOCK), 2 * BLOCK), :]
        kern[n] = dot(tables[...], taps)
        return 0

    lax.fori_loop(0, TAPS + 1, spectrum, 0)
    for q in range(CHUNKS):
        zbuf[0, :, cols(q)] = dot(tables[:, :BLOCK], xbuf[q, lag(0), :])

    def begin(i, _):
        re = pl.ds(pl.multiple_of(i * STRIP, STRIP), STRIP)
        im = pl.ds(pl.multiple_of(i * STRIP + BLOCK, STRIP), STRIP)
        kr, ki = kern[0, re, :], kern[0, im, :]
        wr, wi = zbuf[0, re, :], zbuf[0, im, :]
        total[re, :] = kr * wr - ki * wi
        total[im, :] = kr * wi + ki * wr
        return 0

    lax.fori_loop(0, BLOCK // STRIP, begin, 0)
    get_backward.wait()
    get_gates.wait()

    def wpiece(dz, dyh):
        return wbuf.at[seq_at(dz, dyh, 0)]

    def whalf(dz, dyh, lower):
        return wbuf.at[seq_at(dz, dyh, 0), pl.ds(HALF * lower, HALF)]

    w_mate = [[], []]

    def to_mate(dz, dyh):
        w_mate[dyh].append(send(wpiece(dz, dyh), wpiece(dz, dyh), mate, WEIGHT))

    def forward_far(q):
        pl.when(z > 0)(far[q].wait_recv)
        if q not in DIRECT:
            pl.when((yh == 1) & (z > 0))(near[q].start)
        pl.when((k == 1) & (z > 0))(first[q].start)

    def mates(q):
        @pl.when(s >= 2)
        def _():
            near[q].wait_recv()
            second[q].start()

    def convolve(q):
        pl.when((k == 1) | (z > 0))(first[q].wait_recv)
        pl.when(s >= 2)(second[q].wait_recv)
        for n in range(1, TAPS + 1):
            zbuf[n, :, cols(q)] = dot(tables[:, :BLOCK], xbuf[q, lag(n), :])

        def combine(i, _):
            re = pl.ds(pl.multiple_of(i * STRIP, STRIP), STRIP)
            im = pl.ds(pl.multiple_of(i * STRIP + BLOCK, STRIP), STRIP)
            real, imag = total[re, cols(q)], total[im, cols(q)]
            for n in range(1, TAPS + 1):
                kr, ki = kern[n, re, cols(q)], kern[n, im, cols(q)]
                wr, wi = zbuf[n, re, cols(q)], zbuf[n, im, cols(q)]
                real = real + kr * wr - ki * wi
                imag = imag + kr * wi + ki * wr
            ybuf[re, :] = real.astype(jnp.bfloat16)
            ybuf[im, :] = imag.astype(jnp.bfloat16)
            return 0

        lax.fori_loop(0, BLOCK // STRIP, combine, 0)
        now = xbuf[q, lag(0), :].astype(jnp.float32)
        filtered = dot(inverse[...], ybuf[...]) + skip[:, cols(q)] * now
        abuf[c, :, cols(q)] = (gbuf[:, cols(q)].astype(jnp.float32) * filtered).astype(jnp.bfloat16)

    def apiece(q, dyl, dx):
        return abuf.at[chan_at(dyl, dx), :, cols(q)]

    def ahalf(q, dyl, dx, lower):
        return abuf.at[chan_at(dyl, dx), pl.ds(HALF * lower, HALF), cols(q)]

    def same(ref, device, kind=WEIGHT):
        return send(ref, ref, device, kind)

    def gate(ref, device):
        return send(ref, ref, device, GATED)

    a_up, a_down, a_near = [], [], []

    def spread(q):
        a_up.append(gate(apiece(q, 0, 0), x_up))
        a_down.append(gate(apiece(q, 0, 0), x_down))
        a_near.append(gate(apiece(q, 0, 0), y_near))

    a_up2, a_down2, a_nup, a_ndown, a_nfar = [], [], [], [], []

    def relay(q):
        a_up[q].wait_recv()
        a_up2.append(gate(ahalf(q, 0, -1, 0), x_up))
        a_down[q].wait_recv()
        a_down2.append(gate(ahalf(q, 0, 1, 1), x_down))
        a_near[q].wait_recv()
        a_nup.append(gate(apiece(q, 1, 0), x_up))
        a_ndown.append(gate(apiece(q, 1, 0), x_down))

    def relay_far(q):
        if USE_NEAR:
            a_up2[q].wait_recv()
            a_down2[q].wait_recv()
            a_nfar.append([gate(apiece(q, 0, 2), y_near)])
        else:
            a_nup[q].wait_recv()
            up = gate(ahalf(q, 1, -1, 0), x_up)
            a_ndown[q].wait_recv()
            a_nfar.append([up, gate(ahalf(q, 1, 1, 1), x_down)])

    w = {}

    def both(dz, dyh, device, order):
        return [same(whalf(dz, dyh, lower), device) for lower in order]

    def ready(name):
        for copy in w[name]:
            copy.wait_recv()

    def w_own():
        get_weight.wait()
        drain(wbuf.at[0, pl.ds(0, BLOCK - ROWS)], recv_sem.at[SHARE])
        w["up"] = both(0, 0, z_up, (0, 1))
        w["down"] = both(0, 0, z_down, (1, 0))
        to_mate(0, 0)

    def wquarter(i):
        return wbuf.at[seq_at(0, 0, 0), pl.ds(i * QUARTER, QUARTER)]

    def wother(i):
        return wbuf.at[seq_at(0, 1, 0), pl.ds(i * QUARTER, QUARTER)]

    w["far"], w["fup"], w["fdown"] = [], [], []

    def w_cross(i):
        w["far"].append(same(wquarter(i), y_far))

    def w_relay():
        w["down"].pop(0).wait_recv()
        w["down2"] = same(whalf(1, 0, 1), z_down)
        w["up"].pop(0).wait_recv()
        w["up2"] = same(whalf(-1, 0, 0), z_up)

    def w_mates():
        ready("down")
        to_mate(1, 0)
        ready("up")
        to_mate(-1, 0)

    def w_other(i):
        w["far"][i].wait_recv()
        w["fup"].append(same(wother(i), z_up))
        w["fdown"].append(same(wother(i), z_down))
        if i == 3:
            to_mate(0, 1)

    def w_two():
        w["down2"].wait_recv()
        w["up2"].wait_recv()
        to_mate(2, 0)

    def wnext(dz, i):
        return wbuf.at[seq_at(dz, 1, 0), pl.ds(i * QUARTER, QUARTER)]

    w["fup2"], w["fdown2"] = [], []

    def w_relay_up(i):
        w["fup"][i].wait_recv()
        w["fup2"].append(same(wnext(-1, i), z_up))

    def w_relay_down(i):
        w["fdown"][i].wait_recv()
        w["fdown2"].append(same(wnext(1, i), z_down))

    def w_mates_other():
        for copy in w["fdown"][:2]:
            copy.wait_recv()
        to_mate(1, 1)
        for copy in w["fup"][2:]:
            copy.wait_recv()
        to_mate(-1, 1)

    def w_last():
        for copy in w["fup2"]:
            copy.wait_recv()
        last = [same(whalf(2, 1, 0), mate)]
        for copy in w["fdown2"]:
            copy.wait_recv()
        last.append(same(whalf(2, 1, 1), mate))
        for copy in last:
            copy.wait_recv()

    for step in SCHEDULE:
        name, *rest = step
        {
            "f": forward_far, "n": mates, "c": convolve, "s": spread, "r": relay, "R": relay_far,
            "own": w_own, "x": w_cross, "wr": w_relay, "o": w_other, "w2": w_two,
            "u": w_relay_up, "d": w_relay_down, "wm": w_mates, "wmo": w_mates_other,
        }[name](*rest)
    def project(origin):
        acc[...] += dot(abuf[origin], wbuf[pl.ds(2 * origin, 2)].reshape(WIDTH, WIDTH))

    assert used["send"] <= SENDS and used["recv"] <= ARRIVALS, used
    acc[...] = jnp.zeros_like(acc)
    last_a = chan_at(1, 2)
    last_w = seq_at(2, 1, 0) // 2

    def group(first):
        for step in (0, 2):
            origin = first + step
            pl.when((origin != last_a) & (origin != last_w))(functools.partial(project, origin))

    def wait_all(copies):
        for copy in copies:
            copy.wait_recv()

    wait_all(w_mate[0])
    group(4 * yl + yh)
    wait_all(w_mate[1])
    group(4 * yl + 1 - yh)
    wait_all(a_nup + a_ndown)
    group(4 * (1 - yl) + yh)
    group(4 * (1 - yl) + 1 - yh)
    for copies in a_nfar:
        wait_all(copies)
    pl.when(last_a != last_w)(functools.partial(project, last_a))
    w_last()
    project(last_w)
    obuf[...] = acc[...].astype(jnp.bfloat16)
    mine = pltpu.make_async_copy(
        obuf.at[rows_of(c)], out.at[:, wcols(c)], local_sem.at[len(locals_started)]
    )
    mine.start()
    for dyl, dx in others:
        peer = chan_at(dyl, dx)
        send(obuf.at[rows_of(peer)], out.at[:, wcols(c)], chan_dev(peer), RESULT)
    for copy in far:
        pl.when(z < 3)(copy.wait_send)
    for q, copy in enumerate(near):
        started = s + 2 < GROUPS if q in DIRECT else (yh == 0) | (z > 0)
        pl.when(started)(copy.wait_send)
    for copy in first:
        pl.when((k == 0) | (z > 0))(copy.wait_send)
    for copy in second:
        pl.when(s >= 2)(copy.wait_send)
    part = wbuf.at[0, pl.ds(0, BLOCK - ROWS)]
    drain(part, send_sem.at[SHARE])
    drain(wbuf.at[pl.ds(0, 15)], send_sem.at[WEIGHT])
    drain(wbuf.at[pl.ds(0, 7)], send_sem.at[GATED])
    drain(part, send_sem.at[RESULT])
    mine.wait()
    drain(part, recv_sem.at[RESULT])


SENDS = 4 + 4 * CHUNKS
ARRIVALS = 2 + 4 * CHUNKS + 32 + 9 * CHUNKS


def body(values, gates, filters, skip, out_weight):
    forward, backward = dft_tables(BLOCK)
    forward = jnp.asarray(forward, jnp.bfloat16)
    backward = jnp.asarray(backward, jnp.bfloat16)
    anywhere = pl.BlockSpec(memory_space=pl.ANY)
    local = pl.BlockSpec(memory_space=pltpu.VMEM)
    bf16, f32 = jnp.bfloat16, jnp.float32
    return pl.pallas_call(
        kernel,
        out_shape=jax.ShapeDtypeStruct((ROWS, PEERS * WIDTH), bf16),
        in_specs=[anywhere, anywhere, anywhere, local, anywhere, anywhere, anywhere],
        out_specs=anywhere,
        scratch_shapes=[
            pltpu.VMEM((CHUNKS, (TAPS + 1) * BLOCK, PART), bf16),
            pltpu.VMEM((BLOCK, WIDTH), bf16),
            pltpu.VMEM(((TAPS + 2) * BLOCK, WIDTH), bf16),
            pltpu.VMEM((2 * BLOCK, 2 * BLOCK), bf16),
            pltpu.VMEM((BLOCK, 2 * BLOCK), bf16),
            pltpu.VMEM((TAPS + 1, 2 * BLOCK, WIDTH), f32),
            pltpu.VMEM((TAPS + 1, 2 * BLOCK, WIDTH), f32),
            pltpu.VMEM((2 * BLOCK, WIDTH), f32),
            pltpu.VMEM((2 * BLOCK, PART), bf16),
            pltpu.VMEM((PEERS, BLOCK, WIDTH), bf16),
            pltpu.VMEM((GROUPS, BLOCK, WIDTH), bf16),
            pltpu.VMEM((BLOCK, WIDTH), f32),
            pltpu.VMEM((BLOCK, WIDTH), bf16),
            pltpu.SemaphoreType.DMA((SENDS,)),
            pltpu.SemaphoreType.DMA((ARRIVALS,)),
            pltpu.SemaphoreType.DMA((10,)),
        ],
        compiler_params=pltpu.CompilerParams(
            collective_id=0, has_side_effects=True, vmem_limit_bytes=60 * 1024 * 1024
        ),
    )(values, gates, filters, skip.reshape(1, -1), out_weight, forward, backward)


def solution(mesh):
    in_specs = (
        P("seq", "chan"),
        P("seq", "chan"),
        P(None, "chan"),
        P("chan"),
        P(("seq", "chan"), None),
    )
    out_specs = P(("seq", "chan"), None)
    return jax.shard_map(body, mesh=mesh, in_specs=in_specs, out_specs=out_specs, check_vma=False)
```

time: 50.4 us -> 46.2 us (0.917)
  Pallas kernels: 48.1 us -> 43.9 us
    pallas_call x1, Pallas kernels: 48.1 us -> 43.9 us  [body(): pl.pallas_call(kernel, out_shape=jax.ShapeDtypeStruct((ROWS, PEERS * WIDT...]
where the time goes in v3:
time: 46.2 us; the launch traced here: 45.6 us
  Pallas kernels  43.9 us (95%)
  local copies, waits for them, and re-layouts  1.67 us (4%)
    pallas_call x1, Pallas kernels, body(): pl.pallas_call(kernel, out_shape=jax.ShapeDtypeStruct((ROWS, PEERS * WIDT...  43.9 us
    unnamed x1, local copies, waits for them, and re-layouts  1.67 us

profile of v3, /device:TPU:1, one launch (start us, length us, event | category | flops | bytes accessed | tf_op | source)
XLA Modules:
  0.0 45.6 jit_solution(521293529755715512)
XLA Ops:
  0.0 43.9 %shard_map.73 = bf16[32,4096]{1,0:T(8,128)(2,1)} custom-call(bf16[256,512]{1,0:T(8,128)(2,1)} %values.1, bf16[256,512]{1,0:T(8,128)(2,1)} %gates.1, bf16[1024,512]{1,0:T(8,128)(2,1)} %filters.1, f32[1,512]{1,0:T(1,128)} %bitcast.1, bf16[32,4096]{1,0:T(8,128)(2,1)} %weight.1, bf16[512,512]{1,0:T(8,128)(2,1)} %constant.4.clone.forward, ...), custom_call_target="tpu_custom_call" | custom-call | tf_op jit(solution)/shard_map/pallas_call | solution.py:443
  43.9 1.7 %copy.9 = bf16[32,4096]{1,0:T(8,128)(2,1)} copy(bf16[32,4096]{1,0:T(8,128)(2,1)} %shard_map.73) | data formatting | bytes 524288

commit v4 on v3

--- a/solution.py
+++ b/solution.py
@@ -26,12 +26,12 @@
 DIRECT = (0,)
 SCHEDULE = (
     ("f", 0), ("f", 1), ("n", 0), ("own",), ("x", 0), ("f", 2),
-    ("c", 0), ("s", 0), ("f", 3), ("n", 1), ("x", 1), ("c", 1),
-    ("s", 1), ("x", 2), ("n", 2), ("r", 0), ("wr",), ("c", 2),
-    ("s", 2), ("x", 3), ("n", 3), ("o", 0), ("c", 3), ("s", 3),
-    ("r", 1), ("o", 1), ("wm",), ("r", 2), ("o", 2), ("o", 3),
-    ("R", 0), ("u", 0), ("u", 1), ("w2",), ("r", 3), ("R", 1),
-    ("d", 2), ("R", 2), ("d", 3), ("R", 3), ("wmo",),
+    ("c", 0), ("s", 0), ("x", 1), ("f", 3), ("n", 1), ("x", 2),
+    ("c", 1), ("s", 1), ("x", 3), ("n", 2), ("r", 0), ("wr",),
+    ("o", 0), ("c", 2), ("s", 2), ("n", 3), ("o", 1), ("c", 3),
+    ("s", 3), ("r", 1), ("wm",), ("o", 2), ("r", 2), ("o", 3),
+    ("u", 0), ("R", 0), ("u", 1), ("w2",), ("d", 2), ("r", 3),
+    ("R", 1), ("R", 2), ("d", 3), ("R", 3), ("wmo",),
 )
 
 
@@ -139,13 +139,16 @@
     pl.semaphore_wait(barrier, len(sources))
 
     far, near, first, second = [], [], [], []
+    straight = {}
+    for q in DIRECT:
+        straight[q] = message(values.at[:, cols(q)], xbuf.at[q, lag(2)], seq_dev((s + 2) % GROUPS), HALO)
+        pl.when(s + 2 < GROUPS)(straight[q].start)
     for q in range(CHUNKS):
         copy = message(values.at[:, cols(q)], xbuf.at[q, lag(4)], z_up, HALO)
         pl.when(z < 3)(copy.start)
         far.append(copy)
         if q in DIRECT:
-            copy = message(values.at[:, cols(q)], xbuf.at[q, lag(2)], seq_dev((s + 2) % GROUPS), HALO)
-            pl.when(s + 2 < GROUPS)(copy.start)
+            copy = straight[q]
         else:
             src = pl.ds(pl.multiple_of((1 - yh) * TAPS * BLOCK, BLOCK), BLOCK)
             copy = message(xbuf.at[q, src], xbuf.at[q, lag(2)], y_far, HALO)
@@ -364,8 +367,7 @@
         for copy in w["fdown2"]:
             copy.wait_recv()
         last.append(same(whalf(2, 1, 1), mate))
-        for copy in last:
-            copy.wait_recv()
+        return last
 
     for step in SCHEDULE:
         name, *rest = step
@@ -393,6 +395,7 @@
 
     wait_all(w_mate[0])
     group(4 * yl + yh)
+    final = w_last()
     wait_all(w_mate[1])
     group(4 * yl + 1 - yh)
     wait_all(a_nup + a_ndown)
@@ -401,7 +404,7 @@
     for copies in a_nfar:
         wait_all(copies)
     pl.when(last_a != last_w)(functools.partial(project, last_a))
-    w_last()
+    wait_all(final)
     project(last_w)
     obuf[...] = acc[...].astype(jnp.bfloat16)
     mine = pltpu.make_async_copy(

time: 46.2 us -> 45.6 us (0.987)
  no operation moved by 1% of the time
where the time goes in v4:
time: 45.6 us; the launch traced here: 45.4 us
  Pallas kernels  43.8 us (96%)
  local copies, waits for them, and re-layouts  1.67 us (4%)
    pallas_call x1, Pallas kernels, body(): pl.pallas_call(kernel, out_shape=jax.ShapeDtypeStruct((ROWS, PEERS * WIDT...  43.8 us
    unnamed x1, local copies, waits for them, and re-layouts  1.67 us

profile of v4, /device:TPU:1, one launch (start us, length us, event | category | flops | bytes accessed | tf_op | source)
XLA Modules:
  0.0 45.4 jit_solution(15792445754114097431)
XLA Ops:
  0.0 43.8 %shard_map.73 = bf16[32,4096]{1,0:T(8,128)(2,1)} custom-call(bf16[256,512]{1,0:T(8,128)(2,1)} %values.1, bf16[256,512]{1,0:T(8,128)(2,1)} %gates.1, bf16[1024,512]{1,0:T(8,128)(2,1)} %filters.1, f32[1,512]{1,0:T(1,128)} %bitcast.1, bf16[32,4096]{1,0:T(8,128)(2,1)} %weight.1, bf16[512,512]{1,0:T(8,128)(2,1)} %constant.4.clone.forward, ...), custom_call_target="tpu_custom_call" | custom-call | tf_op jit(solution)/shard_map/pallas_call | solution.py:446
  43.8 1.7 %copy.9 = bf16[32,4096]{1,0:T(8,128)(2,1)} copy(bf16[32,4096]{1,0:T(8,128)(2,1)} %shard_map.73) | data formatting | bytes 524288

commit v5 on v4

--- a/solution.py
+++ b/solution.py
@@ -21,8 +21,8 @@
 HALF = BLOCK // 2
 QUARTER = BLOCK // 4
 STRIP = 32
-USE_NEAR = True
-SHARE, RESULT, WEIGHT, GATED, HALO = range(5)
+SHARE, RESULT, WEIGHT, GATED, FAR, FIRST, SECOND, NEAR, STRAIGHT = range(9)
+RELAYED, ACROSS, MATES = 2, 3, 4
 DIRECT = (0,)
 SCHEDULE = (
     ("f", 0), ("f", 1), ("n", 0), ("own",), ("x", 0), ("f", 2),
@@ -76,22 +76,23 @@
     x_up, x_down = chan_dev(chan_at(0, 1)), chan_dev(chan_at(0, -1))
     y_near = chan_dev(chan_at(1, 0))
 
-    used = {"send": 4, "recv": 2}
-
-    def take(name):
-        used[name] += 1
-        return used[name] - 1
-
-    def message(src, dst, device, kind):
-        send_index = take("send") if kind == HALO else kind
-        recv_index = kind if kind in (SHARE, RESULT) else take("recv")
+    used = [6]
+
+    def take():
+        used[0] += 1
+        return used[0] - 1
+
+    def message(src, dst, device, kind, land=None):
+        if kind in (SHARE, RESULT):
+            land = kind
         return pltpu.make_async_remote_copy(
-            src_ref=src, dst_ref=dst, send_sem=send_sem.at[send_index],
-            recv_sem=recv_sem.at[recv_index], device_id=device, device_id_type=MESH,
+            src_ref=src, dst_ref=dst, send_sem=send_sem.at[kind],
+            recv_sem=recv_sem.at[take() if land is None else land],
+            device_id=device, device_id_type=MESH,
         )
 
-    def send(src, dst, device, kind):
-        copy = message(src, dst, device, kind)
+    def send(src, dst, device, kind, land=None):
+        copy = message(src, dst, device, kind, land)
         copy.start()
         return copy
 
@@ -141,23 +142,23 @@
     far, near, first, second = [], [], [], []
     straight = {}
     for q in DIRECT:
-        straight[q] = message(values.at[:, cols(q)], xbuf.at[q, lag(2)], seq_dev((s + 2) % GROUPS), HALO)
+        straight[q] = message(values.at[:, cols(q)], xbuf.at[q, lag(2)], seq_dev((s + 2) % GROUPS), STRAIGHT)
         pl.when(s + 2 < GROUPS)(straight[q].start)
     for q in range(CHUNKS):
-        copy = message(values.at[:, cols(q)], xbuf.at[q, lag(4)], z_up, HALO)
+        copy = message(values.at[:, cols(q)], xbuf.at[q, lag(4)], z_up, FAR)
         pl.when(z < 3)(copy.start)
         far.append(copy)
         if q in DIRECT:
             copy = straight[q]
         else:
             src = pl.ds(pl.multiple_of((1 - yh) * TAPS * BLOCK, BLOCK), BLOCK)
-            copy = message(xbuf.at[q, src], xbuf.at[q, lag(2)], y_far, HALO)
+            copy = message(xbuf.at[q, src], xbuf.at[q, lag(2)], y_far, NEAR)
         near.append(copy)
         src = pl.ds(pl.multiple_of((1 - k) * TAPS * BLOCK, BLOCK), BLOCK)
         dst = pl.ds(pl.multiple_of((3 - 2 * k) * BLOCK, BLOCK), BLOCK)
-        first.append(message(xbuf.at[q, src], xbuf.at[q, dst], mate, HALO))
+        first.append(message(xbuf.at[q, src], xbuf.at[q, dst], mate, FIRST))
         dst = pl.ds(pl.multiple_of((1 + 2 * k) * BLOCK, BLOCK), BLOCK)
-        second.append(message(xbuf.at[q, lag(2)], xbuf.at[q, dst], mate, HALO))
+        second.append(message(xbuf.at[q, lag(2)], xbuf.at[q, dst], mate, SECOND))
     others = [(1, 2), (1, 1), (1, -1), (0, 2), (1, 0), (0, 1), (0, -1)]
     for dyl, dx in others:
         peer = chan_at(dyl, dx)
@@ -206,10 +207,9 @@
     def whalf(dz, dyh, lower):
         return wbuf.at[seq_at(dz, dyh, 0), pl.ds(HALF * lower, HALF)]
 
-    w_mate = [[], []]
 
     def to_mate(dz, dyh):
-        w_mate[dyh].append(send(wpiece(dz, dyh), wpiece(dz, dyh), mate, WEIGHT))
+        send(wpiece(dz, dyh), wpiece(dz, dyh), mate, WEIGHT, MATES + dyh)
 
     def forward_far(q):
         pl.when(z > 0)(far[q].wait_recv)
@@ -256,8 +256,8 @@
     def same(ref, device, kind=WEIGHT):
         return send(ref, ref, device, kind)
 
-    def gate(ref, device):
-        return send(ref, ref, device, GATED)
+    def gate(ref, device, land=None):
+        return send(ref, ref, device, GATED, land)
 
     a_up, a_down, a_near = [], [], []
 
@@ -266,7 +266,7 @@
         a_down.append(gate(apiece(q, 0, 0), x_down))
         a_near.append(gate(apiece(q, 0, 0), y_near))
 
-    a_up2, a_down2, a_nup, a_ndown, a_nfar = [], [], [], [], []
+    a_up2, a_down2 = [], []
 
     def relay(q):
         a_up[q].wait_recv()
@@ -274,19 +274,13 @@
         a_down[q].wait_recv()
         a_down2.append(gate(ahalf(q, 0, 1, 1), x_down))
         a_near[q].wait_recv()
-        a_nup.append(gate(apiece(q, 1, 0), x_up))
-        a_ndown.append(gate(apiece(q, 1, 0), x_down))
+        gate(apiece(q, 1, 0), x_up, RELAYED)
+        gate(apiece(q, 1, 0), x_down, RELAYED)
 
     def relay_far(q):
-        if USE_NEAR:
-            a_up2[q].wait_recv()
-            a_down2[q].wait_recv()
-            a_nfar.append([gate(apiece(q, 0, 2), y_near)])
-        else:
-            a_nup[q].wait_recv()
-            up = gate(ahalf(q, 1, -1, 0), x_up)
-            a_ndown[q].wait_recv()
-            a_nfar.append([up, gate(ahalf(q, 1, 1, 1), x_down)])
+        a_up2[q].wait_recv()
+        a_down2[q].wait_recv()
+        gate(apiece(q, 0, 2), y_near, ACROSS)
 
     w = {}
 
@@ -379,7 +373,7 @@
     def project(origin):
         acc[...] += dot(abuf[origin], wbuf[pl.ds(2 * origin, 2)].reshape(WIDTH, WIDTH))
 
-    assert used["send"] <= SENDS and used["recv"] <= ARRIVALS, used
+    assert used[0] + 2 == ARRIVALS, used
     acc[...] = jnp.zeros_like(acc)
     last_a = chan_at(1, 2)
     last_w = seq_at(2, 1, 0) // 2
@@ -393,16 +387,15 @@
         for copy in copies:
             copy.wait_recv()
 
-    wait_all(w_mate[0])
+    drain(wbuf.at[pl.ds(0, 4)], recv_sem.at[MATES])
     group(4 * yl + yh)
     final = w_last()
-    wait_all(w_mate[1])
+    drain(wbuf.at[pl.ds(0, 3)], recv_sem.at[MATES + 1])
     group(4 * yl + 1 - yh)
-    wait_all(a_nup + a_ndown)
+    drain(wbuf.at[pl.ds(0, 2)], recv_sem.at[RELAYED])
     group(4 * (1 - yl) + yh)
     group(4 * (1 - yl) + 1 - yh)
-    for copies in a_nfar:
-        wait_all(copies)
+    drain(wbuf.at[0], recv_sem.at[ACROSS])
     pl.when(last_a != last_w)(functools.partial(project, last_a))
     wait_all(final)
     project(last_w)
@@ -414,15 +407,15 @@
     for dyl, dx in others:
         peer = chan_at(dyl, dx)
         send(obuf.at[rows_of(peer)], out.at[:, wcols(c)], chan_dev(peer), RESULT)
-    for copy in far:
-        pl.when(z < 3)(copy.wait_send)
-    for q, copy in enumerate(near):
-        started = s + 2 < GROUPS if q in DIRECT else (yh == 0) | (z > 0)
-        pl.when(started)(copy.wait_send)
-    for copy in first:
-        pl.when((k == 0) | (z > 0))(copy.wait_send)
-    for copy in second:
-        pl.when(s >= 2)(copy.wait_send)
+    def settle(condition, kind, rows):
+        pl.when(condition)(lambda: drain(wbuf.at[0, pl.ds(0, rows)], send_sem.at[kind]))
+
+    per = BLOCK // CHUNKS
+    settle(z < 3, FAR, BLOCK)
+    settle((k == 0) | (z > 0), FIRST, BLOCK)
+    settle(s >= 2, SECOND, BLOCK)
+    settle((yh == 0) | (z > 0), NEAR, BLOCK - per * len(DIRECT))
+    settle(s + 2 < GROUPS, STRAIGHT, per * len(DIRECT))
     part = wbuf.at[0, pl.ds(0, BLOCK - ROWS)]
     drain(part, send_sem.at[SHARE])
     drain(wbuf.at[pl.ds(0, 15)], send_sem.at[WEIGHT])
@@ -432,8 +425,8 @@
     drain(part, recv_sem.at[RESULT])
 
 
-SENDS = 4 + 4 * CHUNKS
-ARRIVALS = 2 + 4 * CHUNKS + 32 + 9 * CHUNKS
+SENDS = 9
+ARRIVALS = 6 + 4 * CHUNKS + 24 + 5 * CHUNKS
 
 
 def body(values, gates, filters, skip, out_weight):

time: 45.6 us -> 45.3 us (level)
  no operation moved by 1% of the time
where the time goes in v5:
time: 45.3 us; the launch traced here: 45.2 us
  Pallas kernels  43.5 us (96%)
  local copies, waits for them, and re-layouts  1.67 us (4%)
    pallas_call x1, Pallas kernels, body(): pl.pallas_call(kernel, out_shape=jax.ShapeDtypeStruct((ROWS, PEERS * WIDT...  43.5 us
    unnamed x1, local copies, waits for them, and re-layouts  1.67 us

profile of v5, /device:TPU:1, one launch (start us, length us, event | category | flops | bytes accessed | tf_op | source)
XLA Modules:
  0.0 45.2 jit_solution(9927003302912495023)
XLA Ops:
  0.0 43.5 %shard_map.73 = bf16[32,4096]{1,0:T(8,128)(2,1)} custom-call(bf16[256,512]{1,0:T(8,128)(2,1)} %values.1, bf16[256,512]{1,0:T(8,128)(2,1)} %gates.1, bf16[1024,512]{1,0:T(8,128)(2,1)} %filters.1, f32[1,512]{1,0:T(1,128)} %bitcast.1, bf16[32,4096]{1,0:T(8,128)(2,1)} %weight.1, bf16[512,512]{1,0:T(8,128)(2,1)} %constant.4.clone.forward, ...), custom_call_target="tpu_custom_call" | custom-call | tf_op jit(solution)/shard_map/pallas_call | solution.py:439
  43.5 1.7 %copy.9 = bf16[32,4096]{1,0:T(8,128)(2,1)} copy(bf16[32,4096]{1,0:T(8,128)(2,1)} %shard_map.73) | data formatting | bytes 524288

commit v6 on v5

--- a/solution.py
+++ b/solution.py
@@ -398,8 +398,8 @@
     drain(wbuf.at[0], recv_sem.at[ACROSS])
     pl.when(last_a != last_w)(functools.partial(project, last_a))
     wait_all(final)
-    project(last_w)
-    obuf[...] = acc[...].astype(jnp.bfloat16)
+    term = dot(abuf[last_w], wbuf[pl.ds(2 * last_w, 2)].reshape(WIDTH, WIDTH))
+    obuf[...] = (acc[...] + term).astype(jnp.bfloat16)
     mine = pltpu.make_async_copy(
         obuf.at[rows_of(c)], out.at[:, wcols(c)], local_sem.at[len(locals_started)]
     )

time: 45.3 us -> 45.3 us (level)
  no operation moved by 1% of the time
where the time goes in v6:
time: 45.3 us; the launch traced here: 45.2 us
  Pallas kernels  43.5 us (96%)
  local copies, waits for them, and re-layouts  1.67 us (4%)
    pallas_call x1, Pallas kernels, body(): pl.pallas_call(kernel, out_shape=jax.ShapeDtypeStruct((ROWS, PEERS * WIDT...  43.5 us
    unnamed x1, local copies, waits for them, and re-layouts  1.67 us

profile of v6, /device:TPU:1, one launch (start us, length us, event | category | flops | bytes accessed | tf_op | source)
XLA Modules:
  0.0 45.2 jit_solution(17828446654175273213)
XLA Ops:
  0.0 43.5 %shard_map.73 = bf16[32,4096]{1,0:T(8,128)(2,1)} custom-call(bf16[256,512]{1,0:T(8,128)(2,1)} %values.1, bf16[256,512]{1,0:T(8,128)(2,1)} %gates.1, bf16[1024,512]{1,0:T(8,128)(2,1)} %filters.1, f32[1,512]{1,0:T(1,128)} %bitcast.1, bf16[32,4096]{1,0:T(8,128)(2,1)} %weight.1, bf16[512,512]{1,0:T(8,128)(2,1)} %constant.4.clone.forward, ...), custom_call_target="tpu_custom_call" | custom-call | tf_op jit(solution)/shard_map/pallas_call | solution.py:439
  43.5 1.7 %copy.9 = bf16[32,4096]{1,0:T(8,128)(2,1)} copy(bf16[32,4096]{1,0:T(8,128)(2,1)} %shard_map.73) | data formatting | bytes 524288
